TPU v7x, 512 devices: a whole 4x4x16 slice. The times are simulated.
512 devices in a mesh: dp: 32 (over z, y_lo), tensor: 16 (over y_hi, x, core).
Axes of the slice: x: 4, y: 4 (y_hi: 2, y_lo: 2; y = y_hi * 2 + y_lo), z: 16, core: 2. Of those that a mesh axis runs over, the one named last changes fastest.
Arguments:
- activations: bfloat16 [32768, 8192], P('dp', 'tensor'), may hold values from -6 to 6
- out_grads: bfloat16 [32768, 8192], P('dp', 'tensor'), may hold values from -6 to 6
- proj_in: bfloat16 [8192, 64], P('tensor'), may hold values from -0.0625 to 0.0625
- proj_out: bfloat16 [8192, 64], P('tensor'), may hold values from -0.0625 to 0.0625
- segment_ids: int32 [32, 1024], P('dp'), may hold values from 0 to 23, never falling along the last dimension, each value on 1 to 80 neighbouring positions
- train_logs: bfloat16 [131072, 4096], P('dp', 'tensor'), may hold values from -6 to 6
- doc_ids: int32 [131072], P(('dp', 'tensor')), may hold values from 0 to 255
Outputs:
- scores: float32 [768, 131072], P(None, ('dp', 'tensor'))
- doc_influence: float32 [768, 256], replicated
Inputs may be any that keep to these rules, and one draw needn't show every extreme that they name: `segment_ids`: in each row the example numbers never fall; each of the 24 examples has 1 to 80 tokens, and one has exactly 80.
All inputs are finite; a program needn't handle non-finite values.
Results may differ from a plain program's by a relative error of at most 0.0052.
Values may be sent and summed in bfloat16 or wider, within the bound.
No kernel may reach another device: no remote copies, remote signals or barrier semaphores. Data moves between devices by JAX's collectives and lax.ppermute only.
A program may use at most 64 MiB of HBM per device.

v0:
```python
import math
import jax
import jax.numpy as jnp
from jax import lax
from jax.sharding import PartitionSpec as P

EX_DEV = 24
DOCS = 256


def per_device(activations, out_grads, proj_in, proj_out, segment_ids, train_logs, doc_ids):
    width_parts = lax.axis_size("tensor")
    position = lax.axis_index("tensor")
    tok_rows = activations.shape[0]
    rank = proj_in.shape[1]
    partial_value = jnp.concatenate(
        [
            jnp.dot(activations, proj_in, preferred_element_type=jnp.float32),
            jnp.dot(out_grads, proj_out, preferred_element_type=jnp.float32),
        ],
        axis=1,
    )
    seg_row = segment_ids[0]
    labels = jnp.arange(EX_DEV, dtype=jnp.int32)
    counts = jnp.sum((seg_row[:, None] == labels[None, :]).astype(jnp.float32), axis=0)
    block_rank = rank // width_parts
    summed = lax.psum(partial_value, "tensor").astype(jnp.bfloat16)
    in_proj = summed[:, :rank]
    out_proj = summed[:, rank:]
    own_out = lax.dynamic_slice_in_dim(out_proj, position * block_rank, block_rank, 1)
    member = (seg_row[:, None] == labels[None, :]).astype(jnp.bfloat16)
    masked = (member[:, :, None] * own_out[:, None, :]).reshape(tok_rows, EX_DEV * block_rank)
    log_sums = jnp.einsum("ta,tj->aj", masked, in_proj, preferred_element_type=jnp.float32)
    log_sums = log_sums.reshape(EX_DEV, block_rank * rank)
    query_block = (log_sums / counts[:, None]).astype(jnp.bfloat16)
    train_full = lax.all_to_all(train_logs, "tensor", split_axis=0, concat_axis=1, tiled=True)
    local_rows = train_full.shape[0]
    wide_block = lax.all_gather(query_block, "tensor", axis=1, tiled=True)
    rows = lax.dot_general(
        lax.all_gather(wide_block, "dp", axis=0, tiled=True),
        train_full,
        (((1,), (1,)), ((), ())),
        preferred_element_type=jnp.float32,
    )
    scores = rows * 0.125
    doc_labels = jnp.arange(DOCS, dtype=jnp.int32)
    doc_hot = (doc_ids[:, None] == doc_labels[None, :]).astype(jnp.float32)
    doc_part = jnp.dot(scores, doc_hot, precision=lax.Precision.HIGHEST)
    total_rows = local_rows * lax.axis_size("tensor") * lax.axis_size("dp")
    doc_total = lax.psum(doc_part, ("dp", "tensor"))
    doc_influence = doc_total / math.sqrt(total_rows / DOCS)
    return (scores, doc_influence)


def solution(mesh):
    placed = (
        P("dp", "tensor"),
        P("dp", "tensor"),
        P("tensor", None),
        P("tensor", None),
        P("dp", None),
        P("dp", "tensor"),
        P(("dp", "tensor")),
    )
    return jax.shard_map(
        per_device,
        mesh=mesh,
        in_specs=placed,
        out_specs=(P(None, ("dp", "tensor")), P()),
        check_vma=False,
    )
```

profile of v0, /device:TPU:2, one launch (start us, length us, event | category | flops | bytes accessed | tf_op | source)
XLA Modules:
  0.0 761.5 jit_solution(6124716450737580398)
XLA Ops:
  7.2 0.0 copy-start
  7.2 0.0 all-gather.2.cloned.1.call-start
  7.2 0.9 convert_reduce_fusion
  8.1 0.7 fusion.4
  8.8 0.0 copy-done
  8.8 1.3 fusion.5
  10.1 1.7 fusion.6
  11.8 0.1 pad_maximum_fusion
  11.8 70.0 %all-reduce.4 = bf16[1024,128]{0,1:T(8,128)(2,1)S(1)} all-reduce(f32[1024,128]{0,1:T(8,128)S(1)} %pad_maximum_fusion), channel_id=1, replica_groups=mesh['dp'=32,'tensor'=16] {'tensor'}, use_global_device_ids=true, to_apply=%region_0.0 | all-reduce | flops 131072 | bytes 786432 | tf_op jit(solution)/shard_map/psum | solution.py:27
  81.9 0.1 broadcast_multiply_fusion.1
  82.0 0.1 mul.30
  82.0 0.2 fusion.1
  82.2 0.1 reshape.42
  82.3 0.1 divide_convert_fusion
  82.4 27.0 %all_gather.6 = bf16[24,4096]{1,0:T(8,128)(2,1)} all-gather(bf16[24,256]{1,0:T(8,128)(2,1)S(1)} %divide_convert_fusion), channel_id=1, replica_groups=mesh['dp'=32,'tensor'=16] {'tensor'}, dimensions={1}, use_global_device_ids=true | all-gather | bytes 208896 | tf_op jit(solution)/shard_map/all_gather | solution.py:38
  109.4 0.0 all-gather.2.cloned.1.call-update
  109.4 0.0 all-reduce.3.cloned.1.call-start
  109.4 34.0 %all_to_all.19 = bf16[16,256,256]{2,1,0:T(8,128)(2,1)S(1)} all-to-all(bf16[16,256,256]{2,1,0:T(8,128)(2,1)} %bitcast.15), channel_id=1, replica_groups=mesh['dp'=32,'tensor'=16] {'tensor'}, dimensions={0} | all-to-all | bytes 4194304 | tf_op jit(solution)/shard_map/all_to_all | solution.py:36
  143.5 2.4 copy.12
  145.9 133.8 %all-gather.2.cloned.1.call-done = bf16[768,4096]{1,0:T(8,128)(2,1)} async-done(((bf16[24,4096]{1,0:T(8,128)(2,1)}), bf16[768,4096]{1,0:T(8,128)(2,1)}) %all-gather.2.cloned.1.call-update) | async-done | bytes 6291472 | tf_op jit(solution)/shard_map/all_gather | solution.py:40
  279.7 0.0 copy-start.2
  279.7 5.2 convolution_multiply_fusion
  284.9 0.0 copy-done.2
  284.9 0.0 copy-start.1
  284.9 1.5 fusion
  286.4 0.0 all-reduce.3.cloned.1.call-update
  286.4 466.2 %all-reduce.3.cloned.1.call-done = f32[768,256]{1,0:T(8,128)} async-done(((f32[768,256]{1,0:T(8,128)}), f32[768,256]{1,0:T(8,128)}) %all-reduce.3.cloned.1.call-update) | async-done | bytes 786448 | tf_op jit(solution)/shard_map/psum | solution.py:50
  752.6 2.1 broadcast_multiply_fusion
  754.7 0.0 copy-done.1
  (2 shorter events, 0.0 us)
Async XLA Ops:
  7.2 1.7 copy-start
  7.2 272.5 %all-gather.2.cloned.1.call-start = ((), (), s32[]{:S(2)}) async-start(), calls=%async_computation.1 | async-start | bytes 6488064 | tf_op jit(solution)/shard_map/all_gather | solution.py:40
  109.4 643.2 %all-reduce.3.cloned.1.call-start = ((), (), s32[]{:S(2)}) async-start(), calls=%async_computation.2 | async-start | bytes 1572864 | tf_op jit(solution)/shard_map/psum | solution.py:50
  279.7 5.2 copy-start.2
  284.9 469.8 %copy-start.1 = (f32[768,256]{1,0:T(8,128)}, f32[768,256]{1,0:T(8,128)S(1)}, u32[]{:S(2)}) copy-start(f32[768,256]{1,0:T(8,128)S(1)} %convolution_multiply_fusion) | copy-start | bytes 2359300
Sparse Core Ops, SparseCore 0:
  109.5 170.1 all-gather.1
  286.5 466.0 all-reduce.2
where the time goes:
time: 762 us
  waiting for transfers between devices  600 us (79%)
  blocking collectives  131 us (17%)
  between operations  14.1 us (2%)
  matrix products  9.8 us (1%)
    psum x1, waiting for transfers between devices, per_device(): doc_total = lax.psum(doc_part, ('dp', 'tensor'))  466 us
    all_gather x1, waiting for transfers between devices, per_device(): lax.all_gather(wide_block, 'dp', axis=0, tiled=True)  134 us
    psum x1, blocking collectives, per_device(): summed = lax.psum(partial_value, 'tensor').astype(jnp.bfloat16)  70 us
    all_to_all x1, blocking collectives, per_device(): lax.all_to_all(train_logs, 'tensor', split_axis=0, concat_axis=1, tiled=T...  34 us
    all_gather x1, blocking collectives, per_device(): wide_block = lax.all_gather(query_block, 'tensor', axis=1, tiled=True)  27 us
  transfers between devices with their start and end apart: 2, of which 2 were waited for; matrix products, arithmetic and copies ran while one was open for 0% of the time, Pallas kernels for 0%

commit v1 on v0

--- a/solution.py
+++ b/solution.py
@@ -47,7 +47,7 @@
     doc_hot = (doc_ids[:, None] == doc_labels[None, :]).astype(jnp.float32)
     doc_part = jnp.dot(scores, doc_hot, precision=lax.Precision.HIGHEST)
     total_rows = local_rows * lax.axis_size("tensor") * lax.axis_size("dp")
-    doc_total = lax.psum(doc_part, ("dp", "tensor"))
+    doc_total = lax.psum(lax.psum(doc_part, "dp"), "tensor")
     doc_influence = doc_total / math.sqrt(total_rows / DOCS)
     return (scores, doc_influence)
 

time: 762 us -> 715 us (0.938)
  the two profiles are of different devices: /device:TPU:2 before, /device:TPU:1 now
where the time goes in v1:
time: 715 us
  waiting for transfers between devices  553 us (77%)
  blocking collectives  132 us (18%)
  between operations  13.8 us (2%)
  matrix products  9.8 us (1%)
    psum x2, waiting for transfers between devices, per_device(): doc_total = lax.psum(lax.psum(doc_part, 'dp'), 'tensor')  423 us
    all_gather x1, waiting for transfers between devices, per_device(): lax.all_gather(wide_block, 'dp', axis=0, tiled=True)  130 us
    psum x1, blocking collectives, per_device(): summed = lax.psum(partial_value, 'tensor').astype(jnp.bfloat16)  71 us
    all_to_all x1, blocking collectives, per_device(): lax.all_to_all(train_logs, 'tensor', split_axis=0, concat_axis=1, tiled=T...  33.9 us
    all_gather x1, blocking collectives, per_device(): wide_block = lax.all_gather(query_block, 'tensor', axis=1, tiled=True)  26.8 us
  transfers between devices with their start and end apart: 3, of which 3 were waited for; matrix products, arithmetic and copies ran while one was open for 0% of the time, Pallas kernels for 0%

profile of v1, /device:TPU:1, one launch (start us, length us, event | category | flops | bytes accessed | tf_op | source)
XLA Modules:
  0.0 714.6 jit_solution(17143630948562208611)
XLA Ops:
  7.2 0.0 copy-start
  7.2 0.0 all-gather.2.cloned.1.call-start
  7.2 0.9 convert_reduce_fusion
  8.1 0.7 fusion.4
  8.8 0.0 copy-done
  8.8 1.3 fusion.5
  10.1 1.7 fusion.6
  11.8 0.1 pad_maximum_fusion
  11.8 71.0 %all-reduce.7 = bf16[1024,128]{0,1:T(8,128)(2,1)S(1)} all-reduce(f32[1024,128]{0,1:T(8,128)S(1)} %pad_maximum_fusion), channel_id=1, replica_groups=mesh['dp'=32,'tensor'=16] {'tensor'}, use_global_device_ids=true, to_apply=%region_0.0 | all-reduce | flops 131072 | bytes 786432 | tf_op jit(solution)/shard_map/psum | solution.py:27
  82.9 0.1 broadcast_multiply_fusion.1
  83.0 0.1 mul.30
  83.0 0.2 fusion.1
  83.2 0.1 reshape.42
  83.3 0.1 divide_convert_fusion
  83.4 26.8 %all_gather.6 = bf16[24,4096]{1,0:T(8,128)(2,1)} all-gather(bf16[24,256]{1,0:T(8,128)(2,1)S(1)} %divide_convert_fusion), channel_id=1, replica_groups=mesh['dp'=32,'tensor'=16] {'tensor'}, dimensions={1}, use_global_device_ids=true | all-gather | bytes 208896 | tf_op jit(solution)/shard_map/all_gather | solution.py:38
  110.2 0.0 all-gather.2.cloned.1.call-update
  110.2 0.0 all-reduce.4.cloned.1.call-start
  110.3 33.9 %all_to_all.19 = bf16[16,256,256]{2,1,0:T(8,128)(2,1)S(1)} all-to-all(bf16[16,256,256]{2,1,0:T(8,128)(2,1)} %bitcast.15), channel_id=1, replica_groups=mesh['dp'=32,'tensor'=16] {'tensor'}, dimensions={0} | all-to-all | bytes 4194304 | tf_op jit(solution)/shard_map/all_to_all | solution.py:36
  144.2 2.4 copy.12
  146.6 129.9 %all-gather.2.cloned.1.call-done = bf16[768,4096]{1,0:T(8,128)(2,1)} async-done(((bf16[24,4096]{1,0:T(8,128)(2,1)}), bf16[768,4096]{1,0:T(8,128)(2,1)}) %all-gather.2.cloned.1.call-update) | async-done | bytes 6291472 | tf_op jit(solution)/shard_map/all_gather | solution.py:40
  276.5 0.0 copy-start.2
  276.5 5.2 convolution_multiply_fusion
  281.7 0.0 copy-done.2
  281.7 0.0 copy-start.1
  281.7 1.5 fusion
  283.2 0.0 all-reduce.4.cloned.1.call-update
  283.2 0.0 all-reduce.6.cloned.1.call-start
  283.3 245.1 %all-reduce.4.cloned.1.call-done = f32[768,256]{1,0:T(8,128)} async-done(((f32[768,256]{1,0:T(8,128)}), f32[768,256]{1,0:T(8,128)}) %all-reduce.4.cloned.1.call-update) | async-done | bytes 786448 | tf_op jit(solution)/shard_map/psum | solution.py:50
  528.3 0.0 all-reduce.6.cloned.1.call-update
  528.3 177.7 %all-reduce.6.cloned.1.call-done = f32[768,256]{1,0:T(8,128)} async-done(((f32[768,256]{1,0:T(8,128)}), f32[768,256]{1,0:T(8,128)}) %all-reduce.6.cloned.1.call-update) | async-done | bytes 786448 | tf_op jit(solution)/shard_map/psum | solution.py:50
  706.0 2.1 broadcast_multiply_fusion
  708.1 0.0 copy-done.1
  (2 shorter events, 0.0 us)
Async XLA Ops:
  7.2 1.7 copy-start
  7.2 269.3 %all-gather.2.cloned.1.call-start = ((), (), s32[]{:S(2)}) async-start(), calls=%async_computation.1 | async-start | bytes 6488064 | tf_op jit(solution)/shard_map/all_gather | solution.py:40
  110.2 418.1 %all-reduce.4.cloned.1.call-start = ((), (), s32[]{:S(2)}) async-start(), calls=%async_computation.2 | async-start | bytes 1572864 | tf_op jit(solution)/shard_map/psum | solution.py:50
  276.5 5.2 copy-start.2
  281.7 426.4 %copy-start.1 = (f32[768,256]{1,0:T(8,128)}, f32[768,256]{1,0:T(8,128)S(1)}, u32[]{:S(2)}) copy-start(f32[768,256]{1,0:T(8,128)S(1)} %convolution_multiply_fusion) | copy-start | bytes 2359300
  283.2 422.8 %all-reduce.6.cloned.1.call-start = ((), (), s32[]{:S(2)}) async-start(), calls=%async_computation.3 | async-start | bytes 1572864 | tf_op jit(solution)/shard_map/psum | solution.py:50
Sparse Core Ops, SparseCore 0:
  110.4 166.0 all-gather.1
  283.3 244.9 all-reduce.3
  531.5 174.4 all-reduce.5
